TPU v7x, 32 devices: a whole 2x2x4 slice. The times are simulated.
32 devices in a mesh: parts: 2 (over x), seq: 8 (over z, y), dp: 2 (over core).
Axes of the slice: x: 2, y: 2, z: 4, core: 2. Of those that a mesh axis runs over, the one named last changes fastest.
Arguments:
- activations: bfloat16 [8, 2048, 1024], P(('parts', 'dp'), 'seq'), parts along dimension 0, may hold values from -36 to 36, as said below
- cotangent: bfloat16 [8, 2048, 1024], P(('parts', 'dp'), 'seq'), parts along dimension 0, may hold values from -6 to 6
- conv_one: bfloat16 [1024, 3, 512], P(('seq', 'dp')), may hold values from -0.109375 to 0.109375
- mix_one: bfloat16 [512, 1024], P(('seq', 'dp')), may hold values from -0.25 to 0.25
- conv_two: bfloat16 [1024, 3, 512], P(('seq', 'dp')), may hold values from -0.109375 to 0.109375
- mix_two: bfloat16 [512, 1024], P(('seq', 'dp')), may hold values from -0.25 to 0.25
Outputs:
- input_grad: bfloat16 [8, 2048, 1024], P(('parts', 'dp'), 'seq'), parts along dimension 0
- grad_conv_one: float32 [2048, 3, 512], P(('parts', 'seq', 'dp')), parts along dimension 0
- grad_mix_one: float32 [1024, 1024], P(('parts', 'seq', 'dp')), parts along dimension 0
- grad_conv_two: float32 [2048, 3, 512], P(('parts', 'seq', 'dp')), parts along dimension 0
- grad_mix_two: float32 [1024, 1024], P(('parts', 'seq', 'dp')), parts along dimension 0
There are 2 independent parts, one for each index of `parts`. A program takes and returns all parts, laid end to end along the dimension named above; an argument that names none is the same for every part. Nothing has to cross between parts.
Inputs may be any that keep to these rules, and one draw needn't show every extreme that they name: activations of earlier layers.
All inputs are finite; a program needn't handle non-finite values.
Results may differ from a plain program's by a relative error of at most 0.007.
Values may be sent and summed in bfloat16 or wider, within the bound.
No kernel may reach another device: no remote copies, remote signals or barrier semaphores. Data moves between devices by JAX's collectives and lax.ppermute only.
A program may use at most 128 MiB of HBM per device.

v0:
```python
import jax
import jax.numpy as jnp
from jax import lax
from jax.sharding import PartitionSpec as P

DILATE_ONE = 64
DILATE_TWO = 128


def with_halo(block, sides, width):
    for axis, dim in sides:
        count = lax.axis_size(axis)
        forward = [(i, i + 1) for i in range(count - 1)]
        backward = [(target, source) for source, target in forward]
        low = lax.ppermute(
            lax.slice_in_dim(block, block.shape[dim] - width, None, axis=dim), axis, forward
        )
        high = lax.ppermute(lax.slice_in_dim(block, 0, width, axis=dim), axis, backward)
        block = jnp.concatenate([low, block, high], axis=dim)
    return block


def prenorm(values):
    scale = lax.rsqrt(jnp.mean(values * values, axis=-1, keepdims=True) + 1e-06)
    return jax.nn.gelu(values * scale)


def fetch(conv_w, mix_w):
    return (
        lax.all_gather(conv_w, ("seq", "dp"), axis=0, tiled=True),
        lax.all_gather(mix_w, ("seq", "dp"), axis=0, tiled=True),
    )


def extended(field, dilate):
    return with_halo(field, (("seq", 1),), dilate)


def views_of(padded, dilate, length):
    return [padded[:, tap * dilate : tap * dilate + length] for tap in range(3)]


def forward(inputs, full_conv, full_mix, dilate):
    width = inputs.shape[-1]
    length = inputs.shape[1]
    normed = prenorm(inputs.astype(jnp.float32)).astype(jnp.bfloat16)
    views = views_of(extended(normed, dilate), dilate, length)
    flat_views = [view.reshape(-1, width) for view in views]
    preact = jnp.dot(flat_views[0], full_conv[:, 0, :], preferred_element_type=jnp.float32)
    for tap in range(1, 3):
        preact = preact + jnp.dot(
            flat_views[tap], full_conv[:, tap, :], preferred_element_type=jnp.float32
        )
    hidden = jax.nn.gelu(preact).astype(jnp.bfloat16)
    mixed = inputs.reshape(-1, width).astype(jnp.float32) + jnp.dot(
        hidden, full_mix, preferred_element_type=jnp.float32
    )
    return (mixed.astype(jnp.bfloat16).reshape(inputs.shape), flat_views, preact, hidden)


def backward(
    inputs, flat_views, preact, hidden, upstream, full_conv, full_mix, conv_rows, mix_rows, dilate
):
    width = inputs.shape[-1]
    length = inputs.shape[1]
    middle = full_mix.shape[0]
    flat_up = upstream.reshape(-1, width)
    contract = (((0,), (0,)), ((), ()))
    dhidden = jnp.dot(flat_up, full_mix.T, preferred_element_type=jnp.float32)
    unused, pull = jax.vjp(jax.nn.gelu, preact)
    dpre = pull(dhidden)[0].astype(jnp.bfloat16)
    piece = hidden
    grad_mix = lax.psum_scatter(
        lax.dot_general(piece, flat_up, contract, preferred_element_type=jnp.float32),
        ("seq", "dp"),
        scatter_dimension=0,
        tiled=True,
    )
    terms = []
    for conv_tap in range(3):
        piece = flat_views[conv_tap]
        terms.append(lax.dot_general(piece, dpre, contract, preferred_element_type=jnp.float32))
    grad_conv = lax.psum_scatter(
        jnp.stack(terms, axis=1), ("seq", "dp"), scatter_dimension=0, tiled=True
    )
    dpre_field = dpre.reshape(inputs.shape[0], length, middle)
    back_views = views_of(extended(dpre_field, dilate), dilate, length)
    dnormed = jnp.dot(
        back_views[2].reshape(-1, middle), full_conv[:, 0, :].T, preferred_element_type=jnp.float32
    )
    for tap in range(1, 3):
        dnormed = dnormed + jnp.dot(
            back_views[2 - tap].reshape(-1, middle),
            full_conv[:, tap, :].T,
            preferred_element_type=jnp.float32,
        )
    unused_two, pull_norm = jax.vjp(prenorm, inputs.astype(jnp.float32))
    dinput = pull_norm(dnormed.reshape(inputs.shape))[0]
    result = (upstream.astype(jnp.float32) + dinput).astype(jnp.bfloat16)
    return (result, grad_conv, grad_mix)


def body(activations, cotangent, conv_one, mix_one, conv_two, mix_two):
    conv_full_one, mix_full_one = fetch(conv_one, mix_one)
    second_in, views_one, preact_one, hidden_one = forward(
        activations, conv_full_one, mix_full_one, DILATE_ONE
    )
    conv_full_two, mix_full_two = fetch(conv_two, mix_two)
    unused, views_two, preact_two, hidden_two = forward(
        second_in, conv_full_two, mix_full_two, DILATE_TWO
    )
    conv_back_two, mix_back_two = (conv_full_two, mix_full_two)
    upstream, grad_conv_two, grad_mix_two = backward(
        second_in,
        views_two,
        preact_two,
        hidden_two,
        cotangent,
        conv_back_two,
        mix_back_two,
        conv_two.shape[0],
        mix_two.shape[0],
        DILATE_TWO,
    )
    conv_back_one, mix_back_one = (conv_full_one, mix_full_one)
    input_grad, grad_conv_one, grad_mix_one = backward(
        activations,
        views_one,
        preact_one,
        hidden_one,
        upstream,
        conv_back_one,
        mix_back_one,
        conv_one.shape[0],
        mix_one.shape[0],
        DILATE_ONE,
    )
    return (input_grad, grad_conv_one, grad_mix_one, grad_conv_two, grad_mix_two)


def solution(mesh):
    in_specs = (
        P(("parts", "dp"), "seq", None),
        P(("parts", "dp"), "seq", None),
        P(("seq", "dp"), None, None),
        P(("seq", "dp"), None),
        P(("seq", "dp"), None, None),
        P(("seq", "dp"), None),
    )
    out_specs = (
        P(("parts", "dp"), "seq", None),
        P(("parts", "seq", "dp"), None, None),
        P(("parts", "seq", "dp"), None),
        P(("parts", "seq", "dp"), None, None),
        P(("parts", "seq", "dp"), None),
    )
    return jax.shard_map(body, mesh=mesh, in_specs=in_specs, out_specs=out_specs, check_vma=False)
```

profile of v0, /device:TPU:0, one launch (start us, length us, event | category | flops | bytes accessed | tf_op | source)
XLA Modules:
  0.0 512.4 jit_solution(3078574404284320583)
XLA Ops:
  7.2 0.7 all-gather.7.cloned.1.call-update
  8.0 0.7 all-gather.9.cloned.1.call-update
  8.7 0.7 all-gather.5.cloned.1.call-update
  9.4 0.5 all-gather.11.cloned.1.call-update
  10.0 1.5 fusion.31
  11.5 0.9 fusion.30
  12.4 4.9 collective-permute-start
  17.3 1.3 collective-permute-start.1
  18.6 12.0 %collective-permute-done = bf16[2,64,1024]{2,1,0:T(8,128)(2,1)S(1)} collective-permute-done((bf16[2,64,1024]{2,1,0:T(8,128)(2,1)S(1)}, bf16[2,64,1024]{2,1,0:T(8,128)(2,1)S(1)}, u32[]{:S(2)}, u32[]{:S(2)}) %collective-permute-start) | collective-permute-done | bytes 262176 | tf_op jit(solution)/shard_map/ppermute | solution.py:15
  30.6 1.2 pad_maximum_fusion.5
  31.9 31.0 %all-gather.7.cloned.1.call-done = bf16[1024,3,512]{2,0,1:T(8,128)(2,1)} async-done(((bf16[64,3,512]{2,0,1:T(8,128)(2,1)}), bf16[1024,3,512]{2,0,1:T(8,128)(2,1)}) %all-gather.7.cloned.1.call-update) | async-done | bytes 3145744 | tf_op jit(solution)/shard_map/all_gather | solution.py:30
  62.9 2.1 fusion.60
  65.1 0.7 fusion.58
  66.2 0.7 fusion.41
  67.0 34.9 %all-gather.9.cloned.1.call-done = bf16[512,1024]{1,0:T(8,128)(2,1)} async-done(((bf16[32,1024]{1,0:T(8,128)(2,1)}), bf16[512,1024]{1,0:T(8,128)(2,1)}) %all-gather.9.cloned.1.call-update) | async-done | bytes 1048592 | tf_op jit(solution)/shard_map/all_gather | solution.py:31
  101.8 3.1 fusion.36
  105.0 3.4 fusion.39
  108.3 1.0 copy-done.3
  109.4 1.1 fusion.80
  110.4 3.2 collective-permute-start.2
  113.6 1.3 collective-permute-start.3
  114.9 28.7 %all-gather.5.cloned.1.call-done = bf16[512,1024]{1,0:T(8,128)(2,1)} async-done(((bf16[32,1024]{1,0:T(8,128)(2,1)}), bf16[512,1024]{1,0:T(8,128)(2,1)}) %all-gather.5.cloned.1.call-update) | async-done | bytes 1048592 | tf_op jit(solution)/shard_map/all_gather | solution.py:31
  143.6 2.9 fusion.84
  146.5 43.3 %all-gather.11.cloned.1.call-done = bf16[1024,3,512]{2,0,1:T(8,128)(2,1)} async-done(((bf16[64,3,512]{2,0,1:T(8,128)(2,1)}), bf16[1024,3,512]{2,0,1:T(8,128)(2,1)}) %all-gather.11.cloned.1.call-update) | async-done | bytes 3145744 | tf_op jit(solution)/shard_map/all_gather | solution.py:30
  189.9 2.6 fusion.63
  192.5 1.5 pad_maximum_fusion.3
  194.1 0.6 copy-done.14
  194.7 0.7 fusion.65
  195.4 0.8 copy-done.22
  196.2 1.4 fusion.55
  197.6 2.2 fusion.66
  199.9 2.5 collective-permute-start.5
  202.4 1.7 collective-permute-start.4
  204.2 2.0 fusion.62
  206.1 2.2 collective-permute-done.5
  208.4 5.5 %collective-permute-done.4 = bf16[2,128,512]{2,1,0:T(8,128)(2,1)S(1)} collective-permute-done((bf16[2,128,512]{2,1,0:T(8,128)(2,1)S(1)}, bf16[2,128,512]{2,1,0:T(8,128)(2,1)S(1)}, u32[]{:S(2)}, u32[]{:S(2)}) %collective-permute-start.4) | collective-permute-done | bytes 262176 | tf_op jit(solution)/shard_map/ppermute | solution.py:18
  213.9 0.7 fusion.61
  214.7 0.5 copy-done.20
  215.1 3.3 fusion.20
  218.5 3.8 fusion.22
  222.4 1.0 copy-done.12
  223.3 2.2 fusion.77
  225.6 2.2 convolution_bitcast_fusion
  227.9 0.7 convolution_bitcast_fusion.2
  228.6 0.5 copy-done.21
  229.1 1.2 convolution_bitcast_fusion.1
  230.3 3.4 pad_maximum_fusion.1
  233.8 3.2 fusion.48
  237.0 0.8 convolution_bitcast_fusion.3
  237.8 0.7 convolution_bitcast_fusion.4
  238.5 0.5 copy-done.2
  239.0 0.7 convolution_bitcast_fusion.5
  239.7 3.4 pad_maximum_fusion
  243.1 4.4 collective-permute-start.7
  247.5 1.8 collective-permute-start.6
  249.3 2.0 fusion.57
  251.3 5.5 %collective-permute-done.6 = bf16[2,64,512]{2,1,0:T(8,128)(2,1)S(1)} collective-permute-done((bf16[2,64,512]{2,1,0:T(8,128)(2,1)S(1)}, bf16[2,64,512]{2,1,0:T(8,128)(2,1)S(1)}, u32[]{:S(2)}, u32[]{:S(2)}) %collective-permute-start.6) | collective-permute-done | bytes 131104 | tf_op jit(solution)/shard_map/ppermute | solution.py:18
  256.8 0.7 fusion.56
  257.6 0.7 add_add_fusion.2
  258.3 1.9 fusion.32
  260.3 3.0 fusion.24
  263.3 63.9 %reduce-scatter.7.cloned.1.call-done = f32[32,1024]{1,0:T(8,128)} async-done(((f32[512,1024]{1,0:T(8,128)}), f32[32,1024]{1,0:T(8,128)}) %reduce-scatter.7.cloned.1.call-update) | async-done | bytes 131088 | tf_op jit(solution)/shard_map/reduce_scatter | solution.py:73
  327.2 88.8 %reduce-scatter.9.cloned.1.call-done = f32[64,3,512]{2,0,1:T(8,128)} async-done(((f32[1024,3,512]{2,0,1:T(8,128)}), f32[64,3,512]{2,0,1:T(8,128)}) %reduce-scatter.9.cloned.1.call-update) | async-done | bytes 393232 | tf_op jit(solution)/shard_map/reduce_scatter | solution.py:83
  416.0 89.6 %reduce-scatter.5.cloned.1.call-done = f32[64,3,512]{2,0,1:T(8,128)} async-done(((f32[1024,3,512]{2,0,1:T(8,128)}), f32[64,3,512]{2,0,1:T(8,128)}) %reduce-scatter.5.cloned.1.call-update) | async-done | bytes 393232 | tf_op jit(solution)/shard_map/reduce_scatter | solution.py:83
  (68 shorter events, 1.3 us)
Async XLA Ops:
  7.2 4.4 copy-start
  7.2 55.7 %all-gather.7.cloned.1.call-start = ((), (), s32[]{:S(2)}) async-start(), calls=%async_computation.5 | async-start | bytes 3342336 | tf_op jit(solution)/shard_map/all_gather | solution.py:30
  7.9 93.9 %all-gather.9.cloned.1.call-start = ((), (), s32[]{:S(2)}) async-start(), calls=%async_computation.6 | async-start | bytes 1114112 | tf_op jit(solution)/shard_map/all_gather | solution.py:31
  8.7 134.9 %all-gather.5.cloned.1.call-start = ((), (), s32[]{:S(2)}) async-start(), calls=%async_computation.4 | async-start | bytes 1114112 | tf_op jit(solution)/shard_map/all_gather | solution.py:31
  9.4 180.5 %all-gather.11.cloned.1.call-start = ((), (), s32[]{:S(2)}) async-start(), calls=%async_computation.7 | async-start | bytes 3342336 | tf_op jit(solution)/shard_map/all_gather | solution.py:30
  10.0 253.3 %reduce-scatter.11.cloned.1.call-start = ((), (), s32[]{:S(2)}) async-start(), calls=%async_computation.11 | async-start | bytes 2228224 | tf_op jit(solution)/shard_map/reduce_scatter | solution.py:73
  12.4 18.2 %collective-permute-start = (bf16[2,64,1024]{2,1,0:T(8,128)(2,1)S(1)}, bf16[2,64,1024]{2,1,0:T(8,128)(2,1)S(1)}, u32[]{:S(2)}, u32[]{:S(2)}) collective-permute-start(bf16[2,64,1024]{2,1,0:T(8,128)(2,1)S(1)} %get-tuple-element.13), channel_id=1, source_target_pairs={{0,2},{2,4},{4,6},{6,8},{8,10},{10,12},{12,14},{1,3},{3,5},{5,7},{... | collective-permute-start | bytes 786440 | tf_op jit(solution)/shard_map/ppermute | solution.py:15
  17.3 13.3 %collective-permute-start.1 = (bf16[2,64,1024]{2,1,0:T(8,128)(2,1)S(1)}, bf16[2,64,1024]{2,1,0:T(8,128)(2,1)S(1)}, u32[]{:S(2)}, u32[]{:S(2)}) collective-permute-start(bf16[2,64,1024]{2,1,0:T(8,128)(2,1)S(1)} %get-tuple-element.14), channel_id=1, source_target_pairs={{2,0},{4,2},{6,4},{8,6},{10,8},{12,10},{14,12},{3,1},{5,3},{7,5},{... | collective-permute-start | bytes 786440 | tf_op jit(solution)/shard_map/ppermute | solution.py:18
  31.9 34.0 %copy-start.7 = (bf16[2,256,1024]{2,1,0:T(8,128)(2,1)}, bf16[2,256,1024]{2,1,0:T(8,128)(2,1)S(1)}, u32[]{:S(2)}) copy-start(bf16[2,256,1024]{2,1,0:T(8,128)(2,1)S(1)} %get-tuple-element.12) | copy-start | bytes 3145732
  62.9 2.2 copy-start.5
  65.0 1.3 copy-start.1
  66.9 38.0 %copy-start.16 = (f32[512,512]{1,0:T(8,128)}, f32[512,512]{1,0:T(8,128)S(1)}, u32[]{:S(2)}) copy-start(f32[512,512]{1,0:T(8,128)S(1)} %fusion.41) | copy-start | bytes 3145732
  108.3 1.0 copy-start.3
  108.3 35.3 %copy-start.18 = (bf16[2,256,1024]{2,1,0:T(8,128)(2,1)S(1)}, bf16[2,256,1024]{2,1,0:T(8,128)(2,1)}, u32[]{:S(2)}) copy-start(bf16[2,256,1024]{2,1,0:T(8,128)(2,1)} %param.7) | copy-start | bytes 3145732
  110.4 82.1 %collective-permute-start.2 = (bf16[2,128,1024]{2,1,0:T(8,128)(2,1)}, bf16[2,128,1024]{2,1,0:T(8,128)(2,1)}, u32[]{:S(2)}, u32[]{:S(2)}) collective-permute-start(bf16[2,128,1024]{2,1,0:T(8,128)(2,1)} %get-tuple-element.9), channel_id=1, source_target_pairs={{0,2},{2,4},{4,6},{6,8},{8,10},{10,12},{12,14},{1,3},{3,5},{5,7},{... | collective-permute-start | bytes 1572872 | tf_op jit(solution)/shard_map/ppermute | solution.py:15
  113.6 78.9 %collective-permute-start.3 = (bf16[2,128,1024]{2,1,0:T(8,128)(2,1)}, bf16[2,128,1024]{2,1,0:T(8,128)(2,1)}, u32[]{:S(2)}, u32[]{:S(2)}) collective-permute-start(bf16[2,128,1024]{2,1,0:T(8,128)(2,1)} %get-tuple-element.10), channel_id=1, source_target_pairs={{2,0},{4,2},{6,4},{8,6},{10,8},{12,10},{14,12},{3,1},{5,3},{7,5},{... | collective-permute-start | bytes 1572872 | tf_op jit(solution)/shard_map/ppermute | solution.py:18
  189.9 2.7 copy-start.4
  192.5 2.2 copy-start.14
  194.1 3.5 copy-start.9
  194.1 3.5 copy-start.11
  194.1 2.1 copy-start.22
  196.2 1.4 copy-start.19
  199.8 127.3 %reduce-scatter.7.cloned.1.call-start = ((), (), s32[]{:S(2)}) async-start(), calls=%async_computation.9 | async-start | bytes 2228224 | tf_op jit(solution)/shard_map/reduce_scatter | solution.py:73
  199.9 8.4 %collective-permute-start.5 = (bf16[2,128,512]{2,1,0:T(8,128)(2,1)S(1)}, bf16[2,128,512]{2,1,0:T(8,128)(2,1)S(1)}, u32[]{:S(2)}, u32[]{:S(2)}) collective-permute-start(bf16[2,128,512]{2,1,0:T(8,128)(2,1)S(1)} %get-tuple-element.21), channel_id=1, source_target_pairs={{0,2},{2,4},{4,6},{6,8},{8,10},{10,12},{12,14},{1,3},{3,5},{5,7},{... | collective-permute-start | bytes 786440 | tf_op jit(solution)/shard_map/ppermute | solution.py:15
  202.4 11.5 %copy-start.15 = (bf16[1024,3,512]{2,0,1:T(8,128)(2,1)S(1)}, bf16[1024,3,512]{2,0,1:T(8,128)(2,1)}, u32[]{:S(2)}) copy-start(bf16[1024,3,512]{2,0,1:T(8,128)(2,1)} %all-gather.11.cloned.1.call-done) | copy-start | bytes 9437188
  202.4 11.4 %collective-permute-start.4 = (bf16[2,128,512]{2,1,0:T(8,128)(2,1)S(1)}, bf16[2,128,512]{2,1,0:T(8,128)(2,1)S(1)}, u32[]{:S(2)}, u32[]{:S(2)}) collective-permute-start(bf16[2,128,512]{2,1,0:T(8,128)(2,1)S(1)} %get-tuple-element.22), channel_id=1, source_target_pairs={{2,0},{4,2},{6,4},{8,6},{10,8},{12,10},{14,12},{3,1},{5,3},{7,5},{... | collective-permute-start | bytes 786440 | tf_op jit(solution)/shard_map/ppermute | solution.py:18
  213.9 1.3 copy-start.20
  218.5 4.8 copy-start.17
  222.4 1.0 copy-start.12
  225.5 190.5 %reduce-scatter.9.cloned.1.call-start = ((), (), s32[]{:S(2)}) async-start(), calls=%async_computation.10 | async-start | bytes 6684672 | tf_op jit(solution)/shard_map/reduce_scatter | solution.py:83
  225.6 2.3 copy-start.10
  227.9 1.2 copy-start.21
  233.7 271.9 %reduce-scatter.5.cloned.1.call-start = ((), (), s32[]{:S(2)}) async-start(), calls=%async_computation.8 | async-start | bytes 6684672 | tf_op jit(solution)/shard_map/reduce_scatter | solution.py:83
  233.8 3.2 copy-start.8
  237.7 1.2 copy-start.2
  243.1 8.1 %collective-permute-start.7 = (bf16[2,64,512]{2,1,0:T(8,128)(2,1)S(1)}, bf16[2,64,512]{2,1,0:T(8,128)(2,1)S(1)}, u32[]{:S(2)}, u32[]{:S(2)}) collective-permute-start(bf16[2,64,512]{2,1,0:T(8,128)(2,1)S(1)} %get-tuple-element.17), channel_id=1, source_target_pairs={{0,2},{2,4},{4,6},{6,8},{8,10},{10,12},{12,14},{1,3},{3,5},{5,7},{... | collective-permute-start | bytes 393224 | tf_op jit(solution)/shard_map/ppermute | solution.py:15
  247.5 9.3 %copy-start.6 = (bf16[1024,3,512]{2,0,1:T(8,128)(2,1)S(1)}, bf16[1024,3,512]{2,0,1:T(8,128)(2,1)}, u32[]{:S(2)}) copy-start(bf16[1024,3,512]{2,0,1:T(8,128)(2,1)} %all-gather.7.cloned.1.call-done) | copy-start | bytes 9437188
  247.5 9.2 %collective-permute-start.6 = (bf16[2,64,512]{2,1,0:T(8,128)(2,1)S(1)}, bf16[2,64,512]{2,1,0:T(8,128)(2,1)S(1)}, u32[]{:S(2)}, u32[]{:S(2)}) collective-permute-start(bf16[2,64,512]{2,1,0:T(8,128)(2,1)S(1)} %get-tuple-element.18), channel_id=1, source_target_pairs={{2,0},{4,2},{6,4},{8,6},{10,8},{12,10},{14,12},{3,1},{5,3},{7,5},{... | collective-permute-start | bytes 393224 | tf_op jit(solution)/shard_map/ppermute | solution.py:18
  258.3 1.9 copy-start.13
Sparse Core Ops, SparseCore 0:
  10.2 52.6 all-gather.6
  65.0 36.7 all-gather.8
  104.0 39.5 all-gather.4
  145.6 44.1 all-gather.10
  199.9 62.3 reduce-scatter.10
  266.9 60.1 reduce-scatter.6
  331.7 84.2 reduce-scatter.8
  421.0 84.4 reduce-scatter.4
where the time goes:
time: 513 us; the launch traced here: 512 us
  waiting for transfers between devices  408 us (80%)
  matrix products  37.7 us (7%)
  other arithmetic  24.2 us (5%)
  starting transfers between devices  21.4 us (4%)
  between operations  14.6 us (3%)
  local copies, waits for them, and re-layouts  6.65 us (1%)
    reduce_scatter x2, waiting for transfers between devices, backward(): lax.psum_scatter(jnp.stack(terms, axis=1), ('seq', 'dp'), scatter_dimensi...  178 us
    all_gather x2, waiting for transfers between devices, fetch(): lax.all_gather(conv_w, ('seq', 'dp'), axis=0, tiled=True)  74.3 us
    reduce_scatter x2, waiting for transfers between devices, backward(): lax.psum_scatter(lax.dot_general(piece, flat_up, contract, preferred_elem...  63.9 us
    all_gather x2, waiting for transfers between devices, fetch(): lax.all_gather(mix_w, ('seq', 'dp'), axis=0, tiled=True)  63.6 us
    ppermute x4, starting transfers between devices, with_halo(): lax.ppermute(lax.slice_in_dim(block, block.shape[dim] - width, None, axis...  15 us
    ppermute x4, waiting for transfers between devices, with_halo(): lax.ppermute(lax.slice_in_dim(block, block.shape[dim] - width, None, axis...  14.2 us
    ppermute x4, waiting for transfers between devices, with_halo(): lax.ppermute(lax.slice_in_dim(block, 0, width, axis=dim), axis, backward)  10.9 us
  transfers between devices with their start and end apart: 16, of which 11 were waited for; matrix products, arithmetic and copies ran while one was open for 11% of the time, Pallas kernels for 0%

commit v1 on v0

--- a/solution.py
+++ b/solution.py
@@ -1,10 +1,32 @@
+import functools
 import jax
 import jax.numpy as jnp
 from jax import lax
 from jax.sharding import PartitionSpec as P
+from jax.lax import axis_index, axis_size, ppermute
 
 DILATE_ONE = 64
 DILATE_TWO = 128
+
+
+def take_shifts_all(mine_x, peer_axis):
+    items = []
+    workers = axis_size(peer_axis)
+    for kk in range(workers):
+        items.append((kk, (kk + 1) % workers))
+    queue = []
+    for kk in range(workers):
+        queue.append((kk, (kk - 1) % workers))
+    work_now, r1 = ([mine_x], [mine_x])
+    for _ in range(workers // 2):
+        work_now.append(ppermute(work_now[-1], peer_axis, items))
+    for _ in range((workers - 1) // 2):
+        r1.append(ppermute(r1[-1], peer_axis, queue))
+    block_now = jnp.concatenate([*work_now[::-1], *r1[1:]], axis=0)
+    return jnp.roll(block_now, (axis_index(peer_axis) - workers // 2) * mine_x.shape[0], axis=0)
+
+
+_review_trees = functools.partial(take_shifts_all, peer_axis=("seq", "dp"))
 
 
 def with_halo(block, sides, width):
@@ -26,10 +48,7 @@
 
 
 def fetch(conv_w, mix_w):
-    return (
-        lax.all_gather(conv_w, ("seq", "dp"), axis=0, tiled=True),
-        lax.all_gather(mix_w, ("seq", "dp"), axis=0, tiled=True),
-    )
+    return (lax.all_gather(conv_w, ("seq", "dp"), axis=0, tiled=True), _review_trees(mix_w))
 
 
 def extended(field, dilate):

time: 513 us -> 458 us (0.89)
  waiting for transfers between devices: 408 us -> 275 us
  starting transfers between devices: 21.4 us -> 75.1 us
  local copies, waits for them, and re-layouts: 6.65 us -> 32 us
    all_gather x2, waiting for transfers between devices: 74.3 us -> 0.01 us  [fetch(): lax.all_gather(conv_w, ('seq', 'dp'), axis=0, tiled=True)]
    all_gather x2 -> x0, waiting for transfers between devices: 63.6 us -> none  [fetch(): lax.all_gather(mix_w, ('seq', 'dp'), axis=0, tiled=True)]
    ppermute x0 -> x30, starting transfers between devices: none -> 56.9 us  [the longest x14 47.9 us: take_shifts_all(): r1.append(ppermute(r1[-1], peer_axis, queue))]
    unnamed x46 -> x100, local copies, waits for them, and re-layouts: 5.46 us -> 28.6 us
    ppermute x4, waiting for transfers between devices: 14.2 us -> 23.5 us  [with_halo(): lax.ppermute(lax.slice_in_dim(block, block.shape[dim] - width, None, axis...]
    ppermute x4, waiting for transfers between devices: 10.9 us -> 3.59 us  [with_halo(): lax.ppermute(lax.slice_in_dim(block, 0, width, axis=dim), axis, backward)]
    ppermute x0 -> x30, waiting for transfers between devices: none -> 6.94 us  [the longest x16 6.37 us: take_shifts_all(): work_now.append(ppermute(work_now[-1], peer_axis, items))]
  transfers between devices with their start and end apart: 16 -> 44, of which waited for: 11 -> 14; matrix products, arithmetic and copies ran while one was open for 11% -> 18% of each run, Pallas kernels for 0% -> 0%
where the time goes in v1:
time: 458 us; the launch traced here: 457 us
  waiting for transfers between devices  275 us (60%)
  starting transfers between devices  75.1 us (16%)
  matrix products  35.8 us (8%)
  local copies, waits for them, and re-layouts  32 us (7%)
  other arithmetic  24.2 us (5%)
  between operations  14.8 us (3%)
    reduce_scatter x2, waiting for transfers between devices, backward(): lax.psum_scatter(jnp.stack(terms, axis=1), ('seq', 'dp'), scatter_dimensi...  178 us
    reduce_scatter x2, waiting for transfers between devices, backward(): lax.psum_scatter(lax.dot_general(piece, flat_up, contract, preferred_elem...  62 us
    ppermute x14, starting transfers between devices, take_shifts_all(): r1.append(ppermute(r1[-1], peer_axis, queue))  47.9 us
    unnamed x100, local copies, waits for them, and re-layouts  28.6 us
    ppermute x4, waiting for transfers between devices, with_halo(): lax.ppermute(lax.slice_in_dim(block, block.shape[dim] - width, None, axis...  23.5 us
    ppermute x4, starting transfers between devices, with_halo(): lax.ppermute(lax.slice_in_dim(block, block.shape[dim] - width, None, axis...  12.2 us
  transfers between devices with their start and end apart: 44, of which 14 were waited for; matrix products, arithmetic and copies ran while one was open for 18% of the time, Pallas kernels for 0%

profile of v1, /device:TPU:0, one launch (start us, length us, event | category | flops | bytes accessed | tf_op | source)
XLA Modules:
  0.0 456.6 jit_solution(3405056509146850486)
XLA Ops:
  8.4 5.1 %collective-permute-start.25 = (bf16[32,1024]{1,0:T(8,128)(2,1)}, bf16[32,1024]{1,0:T(8,128)(2,1)S(1)}, u32[]{:S(2)}, u32[]{:S(2)}) collective-permute-start(bf16[32,1024]{1,0:T(8,128)(2,1)} %param.11), channel_id=1, source_target_pairs={{0,15},{1,0},{2,1},{3,2},{4,3},{5,4},{6,5},{7,6},{8,7},{9,8},{10,9... | collective-permute-start | bytes 196616 | tf_op jit(solution)/shard_map/ppermute | solution.py:24
  13.5 4.4 collective-permute-start.8
  18.0 1.5 fusion.31
  19.5 2.1 fusion.30
  21.7 4.4 collective-permute-start.26
  26.1 1.3 collective-permute-start.15
  27.5 4.4 collective-permute-start.9
  32.0 4.4 collective-permute-start.27
  36.4 4.4 collective-permute-start.10
  40.9 1.3 collective-permute-start.16
  42.8 3.9 collective-permute-start.28
  46.7 1.6 collective-permute-done.20
  48.9 4.6 %collective-permute-start.11 = (bf16[32,1024]{1,0:T(8,128)(2,1)S(1)}, bf16[32,1024]{1,0:T(8,128)(2,1)S(1)}, u32[]{:S(2)}, u32[]{:S(2)}) collective-permute-start(bf16[32,1024]{1,0:T(8,128)(2,1)S(1)} %collective-permute-done.10), channel_id=1, source_target_pairs={{0,15},{1,0},{2,1},{3,2},{4,3},{5,4},{6,5},{7,6},{8,7},{9,8},{10,9... | collective-permute-start | bytes 196616 | tf_op jit(solution)/shard_map/ppermute | solution.py:24
  54.1 5.6 %collective-permute-start.4 = (bf16[32,1024]{1,0:T(8,128)(2,1)S(1)}, bf16[32,1024]{1,0:T(8,128)(2,1)S(1)}, u32[]{:S(2)}, u32[]{:S(2)}) collective-permute-start(bf16[32,1024]{1,0:T(8,128)(2,1)S(1)} %collective-permute-done.3), channel_id=1, source_target_pairs={{0,1},{1,2},{2,3},{3,4},{4,5},{5,6},{6,7},{7,8},{8,9},{9,10},{10,1... | collective-permute-start | bytes 196616 | tf_op jit(solution)/shard_map/ppermute | solution.py:22
  59.7 1.7 collective-permute-start.22
  61.4 2.8 collective-permute-start.29
  64.7 1.7 collective-permute-done.22
  66.6 4.5 collective-permute-start.30
  71.6 1.3 collective-permute-done.23
  73.0 1.3 pad_maximum_fusion.5
  74.3 4.4 collective-permute-start.31
  80.3 1.5 constant_dynamic-update-slice_fusion.30
  87.5 1.5 constant_dynamic-update-slice_fusion.13
  95.2 1.5 constant_dynamic-update-slice_fusion.18
  99.8 1.5 constant_dynamic-update-slice_fusion.2
  101.9 2.1 fusion.65
  106.5 2.9 fusion.36
  109.5 2.2 fusion.39
  111.7 1.0 copy-done.5
  112.6 1.1 fusion.92
  113.8 2.1 collective-permute-start.32
  115.8 1.5 collective-permute-start.33
  117.3 1.5 constant_dynamic-update-slice_fusion.1
  118.8 1.5 constant_dynamic-update-slice_fusion
  120.2 2.3 fusion.68
  122.6 15.2 %collective-permute-done.32 = bf16[2,128,1024]{2,1,0:T(8,128)(2,1)} collective-permute-done((bf16[2,128,1024]{2,1,0:T(8,128)(2,1)}, bf16[2,128,1024]{2,1,0:T(8,128)(2,1)}, u32[]{:S(2)}, u32[]{:S(2)}) %collective-permute-start.32) | collective-permute-done | bytes 524320 | tf_op jit(solution)/shard_map/ppermute | solution.py:37
  137.8 1.4 pad_maximum_fusion.3
  140.7 1.0 copy-done.18
  141.8 2.2 fusion.71
  144.0 3.4 fusion.55
  147.5 4.4 collective-permute-start.35
  151.9 1.3 collective-permute-start.34
  153.9 8.3 %collective-permute-done.35 = bf16[2,128,512]{2,1,0:T(8,128)(2,1)S(1)} collective-permute-done((bf16[2,128,512]{2,1,0:T(8,128)(2,1)S(1)}, bf16[2,128,512]{2,1,0:T(8,128)(2,1)S(1)}, u32[]{:S(2)}, u32[]{:S(2)}) %collective-permute-start.35) | collective-permute-done | bytes 262176 | tf_op jit(solution)/shard_map/ppermute | solution.py:37
  163.5 3.3 fusion.20
  166.9 3.8 fusion.22
  170.7 1.0 copy-done.12
  171.7 2.2 fusion.84
  173.9 2.1 convolution_bitcast_fusion
  176.0 0.7 convolution_bitcast_fusion.2
  177.2 1.2 convolution_bitcast_fusion.1
  178.4 3.3 pad_maximum_fusion.1
  182.1 3.4 fusion.48
  185.5 0.8 convolution_bitcast_fusion.3
  186.2 0.7 convolution_bitcast_fusion.4
  188.2 3.4 pad_maximum_fusion
  191.7 4.4 collective-permute-start.37
  196.1 1.6 collective-permute-start.36
  197.6 2.0 fusion.62
  199.6 3.6 collective-permute-done.36
  204.8 1.9 fusion.32
  206.7 3.0 fusion.24
  209.7 62.0 %reduce-scatter.7.cloned.1.call-done = f32[32,1024]{1,0:T(8,128)} async-done(((f32[512,1024]{1,0:T(8,128)}), f32[32,1024]{1,0:T(8,128)}) %reduce-scatter.7.cloned.1.call-update) | async-done | bytes 131088 | tf_op jit(solution)/shard_map/reduce_scatter | solution.py:92
  271.8 88.7 %reduce-scatter.9.cloned.1.call-done = f32[64,3,512]{2,0,1:T(8,128)} async-done(((f32[1024,3,512]{2,0,1:T(8,128)}), f32[64,3,512]{2,0,1:T(8,128)}) %reduce-scatter.9.cloned.1.call-update) | async-done | bytes 393232 | tf_op jit(solution)/shard_map/reduce_scatter | solution.py:102
  360.4 89.3 %reduce-scatter.5.cloned.1.call-done = f32[64,3,512]{2,0,1:T(8,128)} async-done(((f32[1024,3,512]{2,0,1:T(8,128)}), f32[64,3,512]{2,0,1:T(8,128)}) %reduce-scatter.5.cloned.1.call-update) | async-done | bytes 393232 | tf_op jit(solution)/shard_map/reduce_scatter | solution.py:102
  (178 shorter events, 31.5 us)
Async XLA Ops:
  7.2 94.8 %all-gather.3.cloned.1.call-start = ((), (), s32[]{:S(2)}) async-start(), calls=%async_computation.4 | async-start | bytes 3342336 | tf_op jit(solution)/shard_map/all_gather | solution.py:51
  7.9 112.3 %all-gather.5.cloned.1.call-start = ((), (), s32[]{:S(2)}) async-start(), calls=%async_computation.5 | async-start | bytes 3342336 | tf_op jit(solution)/shard_map/all_gather | solution.py:51
  7.9 13.6 %collective-permute-start.17 = (bf16[32,1024]{1,0:T(8,128)(2,1)}, bf16[32,1024]{1,0:T(8,128)(2,1)S(1)}, u32[]{:S(2)}, u32[]{:S(2)}) collective-permute-start(bf16[32,1024]{1,0:T(8,128)(2,1)} %param.11), channel_id=1, source_target_pairs={{0,1},{1,2},{2,3},{3,4},{4,5},{5,6},{6,7},{7,8},{8,9},{9,10},{10,1... | collective-permute-start | bytes 196616 | tf_op jit(solution)/shard_map/ppermute | solution.py:22
  8.4 13.2 %collective-permute-start.25 = (bf16[32,1024]{1,0:T(8,128)(2,1)}, bf16[32,1024]{1,0:T(8,128)(2,1)S(1)}, u32[]{:S(2)}, u32[]{:S(2)}) collective-permute-start(bf16[32,1024]{1,0:T(8,128)(2,1)} %param.11), channel_id=1, source_target_pairs={{0,15},{1,0},{2,1},{3,2},{4,3},{5,4},{6,5},{7,6},{8,7},{9,8},{10,9... | collective-permute-start | bytes 196616 | tf_op jit(solution)/shard_map/ppermute | solution.py:24
  13.5 13.9 %collective-permute-start = (bf16[32,1024]{1,0:T(8,128)(2,1)}, bf16[32,1024]{1,0:T(8,128)(2,1)S(1)}, u32[]{:S(2)}, u32[]{:S(2)}) collective-permute-start(bf16[32,1024]{1,0:T(8,128)(2,1)} %param.13), channel_id=1, source_target_pairs={{0,1},{1,2},{2,3},{3,4},{4,5},{5,6},{6,7},{7,8},{8,9},{9,10},{10,1... | collective-permute-start | bytes 196616 | tf_op jit(solution)/shard_map/ppermute | solution.py:22
  13.5 14.0 %collective-permute-start.8 = (bf16[32,1024]{1,0:T(8,128)(2,1)}, bf16[32,1024]{1,0:T(8,128)(2,1)S(1)}, u32[]{:S(2)}, u32[]{:S(2)}) collective-permute-start(bf16[32,1024]{1,0:T(8,128)(2,1)} %param.13), channel_id=1, source_target_pairs={{0,15},{1,0},{2,1},{3,2},{4,3},{5,4},{6,5},{7,6},{8,7},{9,8},{10,9... | collective-permute-start | bytes 196616 | tf_op jit(solution)/shard_map/ppermute | solution.py:24
  21.6 10.4 %collective-permute-start.18 = (bf16[32,1024]{1,0:T(8,128)(2,1)S(1)}, bf16[32,1024]{1,0:T(8,128)(2,1)S(1)}, u32[]{:S(2)}, u32[]{:S(2)}) collective-permute-start(bf16[32,1024]{1,0:T(8,128)(2,1)S(1)} %collective-permute-done.17), channel_id=1, source_target_pairs={{0,1},{1,2},{2,3},{3,4},{4,5},{5,6},{6,7},{7,8},{8,9},{9,10},{10,1... | collective-permute-start | bytes 196616 | tf_op jit(solution)/shard_map/ppermute | solution.py:22
  21.7 10.3 %collective-permute-start.26 = (bf16[32,1024]{1,0:T(8,128)(2,1)S(1)}, bf16[32,1024]{1,0:T(8,128)(2,1)S(1)}, u32[]{:S(2)}, u32[]{:S(2)}) collective-permute-start(bf16[32,1024]{1,0:T(8,128)(2,1)S(1)} %collective-permute-done.25), channel_id=1, source_target_pairs={{0,15},{1,0},{2,1},{3,2},{4,3},{5,4},{6,5},{7,6},{8,7},{9,8},{10,9... | collective-permute-start | bytes 196616 | tf_op jit(solution)/shard_map/ppermute | solution.py:24
  26.1 35.3 %collective-permute-start.15 = (bf16[2,64,1024]{2,1,0:T(8,128)(2,1)S(1)}, bf16[2,64,1024]{2,1,0:T(8,128)(2,1)S(1)}, u32[]{:S(2)}, u32[]{:S(2)}) collective-permute-start(bf16[2,64,1024]{2,1,0:T(8,128)(2,1)S(1)} %get-tuple-element.14), channel_id=1, source_target_pairs={{0,2},{2,4},{4,6},{6,8},{8,10},{10,12},{12,14},{1,3},{3,5},{5,7},{... | collective-permute-start | bytes 786440 | tf_op jit(solution)/shard_map/ppermute | solution.py:37
  27.4 9.0 %collective-permute-start.1 = (bf16[32,1024]{1,0:T(8,128)(2,1)S(1)}, bf16[32,1024]{1,0:T(8,128)(2,1)S(1)}, u32[]{:S(2)}, u32[]{:S(2)}) collective-permute-start(bf16[32,1024]{1,0:T(8,128)(2,1)S(1)} %collective-permute-done), channel_id=1, source_target_pairs={{0,1},{1,2},{2,3},{3,4},{4,5},{5,6},{6,7},{7,8},{8,9},{9,10},{10,1... | collective-permute-start | bytes 196616 | tf_op jit(solution)/shard_map/ppermute | solution.py:22
  27.5 8.9 %collective-permute-start.9 = (bf16[32,1024]{1,0:T(8,128)(2,1)S(1)}, bf16[32,1024]{1,0:T(8,128)(2,1)S(1)}, u32[]{:S(2)}, u32[]{:S(2)}) collective-permute-start(bf16[32,1024]{1,0:T(8,128)(2,1)S(1)} %collective-permute-done.8), channel_id=1, source_target_pairs={{0,15},{1,0},{2,1},{3,2},{4,3},{5,4},{6,5},{7,6},{8,7},{9,8},{10,9... | collective-permute-start | bytes 196616 | tf_op jit(solution)/shard_map/ppermute | solution.py:24
  31.9 8.9 %collective-permute-start.19 = (bf16[32,1024]{1,0:T(8,128)(2,1)S(1)}, bf16[32,1024]{1,0:T(8,128)(2,1)S(1)}, u32[]{:S(2)}, u32[]{:S(2)}) collective-permute-start(bf16[32,1024]{1,0:T(8,128)(2,1)S(1)} %collective-permute-done.18), channel_id=1, source_target_pairs={{0,1},{1,2},{2,3},{3,4},{4,5},{5,6},{6,7},{7,8},{8,9},{9,10},{10,1... | collective-permute-start | bytes 196616 | tf_op jit(solution)/shard_map/ppermute | solution.py:22
  32.0 8.9 %collective-permute-start.27 = (bf16[32,1024]{1,0:T(8,128)(2,1)S(1)}, bf16[32,1024]{1,0:T(8,128)(2,1)S(1)}, u32[]{:S(2)}, u32[]{:S(2)}) collective-permute-start(bf16[32,1024]{1,0:T(8,128)(2,1)S(1)} %collective-permute-done.26), channel_id=1, source_target_pairs={{0,15},{1,0},{2,1},{3,2},{4,3},{5,4},{6,5},{7,6},{8,7},{9,8},{10,9... | collective-permute-start | bytes 196616 | tf_op jit(solution)/shard_map/ppermute | solution.py:24
  36.4 6.4 %collective-permute-start.2 = (bf16[32,1024]{1,0:T(8,128)(2,1)S(1)}, bf16[32,1024]{1,0:T(8,128)(2,1)S(1)}, u32[]{:S(2)}, u32[]{:S(2)}) collective-permute-start(bf16[32,1024]{1,0:T(8,128)(2,1)S(1)} %collective-permute-done.1), channel_id=1, source_target_pairs={{0,1},{1,2},{2,3},{3,4},{4,5},{5,6},{6,7},{7,8},{8,9},{9,10},{10,1... | collective-permute-start | bytes 196616 | tf_op jit(solution)/shard_map/ppermute | solution.py:22
  36.4 10.3 %collective-permute-start.10 = (bf16[32,1024]{1,0:T(8,128)(2,1)S(1)}, bf16[32,1024]{1,0:T(8,128)(2,1)S(1)}, u32[]{:S(2)}, u32[]{:S(2)}) collective-permute-start(bf16[32,1024]{1,0:T(8,128)(2,1)S(1)} %collective-permute-done.9), channel_id=1, source_target_pairs={{0,15},{1,0},{2,1},{3,2},{4,3},{5,4},{6,5},{7,6},{8,7},{9,8},{10,9... | collective-permute-start | bytes 196616 | tf_op jit(solution)/shard_map/ppermute | solution.py:24
  40.9 7.5 %collective-permute-start.20 = (bf16[32,1024]{1,0:T(8,128)(2,1)S(1)}, bf16[32,1024]{1,0:T(8,128)(2,1)S(1)}, u32[]{:S(2)}, u32[]{:S(2)}) collective-permute-start(bf16[32,1024]{1,0:T(8,128)(2,1)S(1)} %collective-permute-done.19), channel_id=1, source_target_pairs={{0,1},{1,2},{2,3},{3,4},{4,5},{5,6},{6,7},{7,8},{8,9},{9,10},{10,1... | collective-permute-start | bytes 196616 | tf_op jit(solution)/shard_map/ppermute | solution.py:22
  40.9 32.1 %collective-permute-start.16 = (bf16[2,64,1024]{2,1,0:T(8,128)(2,1)S(1)}, bf16[2,64,1024]{2,1,0:T(8,128)(2,1)S(1)}, u32[]{:S(2)}, u32[]{:S(2)}) collective-permute-start(bf16[2,64,1024]{2,1,0:T(8,128)(2,1)S(1)} %get-tuple-element.15), channel_id=1, source_target_pairs={{2,0},{4,2},{6,4},{8,6},{10,8},{12,10},{14,12},{3,1},{5,3},{7,5},{... | collective-permute-start | bytes 786440 | tf_op jit(solution)/shard_map/ppermute | solution.py:40
  42.8 6.1 %collective-permute-start.28 = (bf16[32,1024]{1,0:T(8,128)(2,1)S(1)}, bf16[32,1024]{1,0:T(8,128)(2,1)S(1)}, u32[]{:S(2)}, u32[]{:S(2)}) collective-permute-start(bf16[32,1024]{1,0:T(8,128)(2,1)S(1)} %collective-permute-done.27), channel_id=1, source_target_pairs={{0,15},{1,0},{2,1},{3,2},{4,3},{5,4},{6,5},{7,6},{8,7},{9,8},{10,9... | collective-permute-start | bytes 196616 | tf_op jit(solution)/shard_map/ppermute | solution.py:24
  46.7 7.4 %collective-permute-start.3 = (bf16[32,1024]{1,0:T(8,128)(2,1)S(1)}, bf16[32,1024]{1,0:T(8,128)(2,1)S(1)}, u32[]{:S(2)}, u32[]{:S(2)}) collective-permute-start(bf16[32,1024]{1,0:T(8,128)(2,1)S(1)} %collective-permute-done.2), channel_id=1, source_target_pairs={{0,1},{1,2},{2,3},{3,4},{4,5},{5,6},{6,7},{7,8},{8,9},{9,10},{10,1... | collective-permute-start | bytes 196616 | tf_op jit(solution)/shard_map/ppermute | solution.py:22
  48.3 24.6 %copy-start.27 = (bf16[32,1024]{1,0:T(8,128)(2,1)}, bf16[32,1024]{1,0:T(8,128)(2,1)S(1)}, u32[]{:S(2)}) copy-start(bf16[32,1024]{1,0:T(8,128)(2,1)S(1)} %collective-permute-done.20) | copy-start | bytes 196612
  48.3 11.4 %collective-permute-start.21 = (bf16[32,1024]{1,0:T(8,128)(2,1)S(1)}, bf16[32,1024]{1,0:T(8,128)(2,1)S(1)}, u32[]{:S(2)}, u32[]{:S(2)}) collective-permute-start(bf16[32,1024]{1,0:T(8,128)(2,1)S(1)} %collective-permute-done.20), channel_id=1, source_target_pairs={{0,1},{1,2},{2,3},{3,4},{4,5},{5,6},{6,7},{7,8},{8,9},{9,10},{10,1... | collective-permute-start | bytes 196616 | tf_op jit(solution)/shard_map/ppermute | solution.py:22
  48.9 15.3 %collective-permute-start.11 = (bf16[32,1024]{1,0:T(8,128)(2,1)S(1)}, bf16[32,1024]{1,0:T(8,128)(2,1)S(1)}, u32[]{:S(2)}, u32[]{:S(2)}) collective-permute-start(bf16[32,1024]{1,0:T(8,128)(2,1)S(1)} %collective-permute-done.10), channel_id=1, source_target_pairs={{0,15},{1,0},{2,1},{3,2},{4,3},{5,4},{6,5},{7,6},{8,7},{9,8},{10,9... | collective-permute-start | bytes 196616 | tf_op jit(solution)/shard_map/ppermute | solution.py:24
  54.1 18.8 %copy-start.25 = (bf16[32,1024]{1,0:T(8,128)(2,1)}, bf16[32,1024]{1,0:T(8,128)(2,1)S(1)}, u32[]{:S(2)}) copy-start(bf16[32,1024]{1,0:T(8,128)(2,1)S(1)} %collective-permute-done.3) | copy-start | bytes 196612
  54.1 10.1 %collective-permute-start.4 = (bf16[32,1024]{1,0:T(8,128)(2,1)S(1)}, bf16[32,1024]{1,0:T(8,128)(2,1)S(1)}, u32[]{:S(2)}, u32[]{:S(2)}) collective-permute-start(bf16[32,1024]{1,0:T(8,128)(2,1)S(1)} %collective-permute-done.3), channel_id=1, source_target_pairs={{0,1},{1,2},{2,3},{3,4},{4,5},{5,6},{6,7},{7,8},{8,9},{9,10},{10,1... | collective-permute-start | bytes 196616 | tf_op jit(solution)/shard_map/ppermute | solution.py:22
  59.7 13.2 %copy-start.31 = (bf16[32,1024]{1,0:T(8,128)(2,1)}, bf16[32,1024]{1,0:T(8,128)(2,1)S(1)}, u32[]{:S(2)}) copy-start(bf16[32,1024]{1,0:T(8,128)(2,1)S(1)} %collective-permute-done.21) | copy-start | bytes 196612
  59.7 6.7 %collective-permute-start.22 = (bf16[32,1024]{1,0:T(8,128)(2,1)S(1)}, bf16[32,1024]{1,0:T(8,128)(2,1)S(1)}, u32[]{:S(2)}, u32[]{:S(2)}) collective-permute-start(bf16[32,1024]{1,0:T(8,128)(2,1)S(1)} %collective-permute-done.21), channel_id=1, source_target_pairs={{0,1},{1,2},{2,3},{3,4},{4,5},{5,6},{6,7},{7,8},{8,9},{9,10},{10,1... | collective-permute-start | bytes 196616 | tf_op jit(solution)/shard_map/ppermute | solution.py:22
  61.4 5.2 %collective-permute-start.29 = (bf16[32,1024]{1,0:T(8,128)(2,1)S(1)}, bf16[32,1024]{1,0:T(8,128)(2,1)}, u32[]{:S(2)}, u32[]{:S(2)}) collective-permute-start(bf16[32,1024]{1,0:T(8,128)(2,1)S(1)} %collective-permute-done.28), channel_id=1, source_target_pairs={{0,15},{1,0},{2,1},{3,2},{4,3},{5,4},{6,5},{7,6},{8,7},{9,8},{10,9... | collective-permute-start | bytes 196616 | tf_op jit(solution)/shard_map/ppermute | solution.py:24
  64.2 6.9 %collective-permute-start.12 = (bf16[32,1024]{1,0:T(8,128)(2,1)S(1)}, bf16[32,1024]{1,0:T(8,128)(2,1)}, u32[]{:S(2)}, u32[]{:S(2)}) collective-permute-start(bf16[32,1024]{1,0:T(8,128)(2,1)S(1)} %collective-permute-done.11), channel_id=1, source_target_pairs={{0,15},{1,0},{2,1},{3,2},{4,3},{5,4},{6,5},{7,6},{8,7},{9,8},{10,9... | collective-permute-start | bytes 196616 | tf_op jit(solution)/shard_map/ppermute | solution.py:24
  64.2 8.7 %copy-start.29 = (bf16[32,1024]{1,0:T(8,128)(2,1)}, bf16[32,1024]{1,0:T(8,128)(2,1)S(1)}, u32[]{:S(2)}) copy-start(bf16[32,1024]{1,0:T(8,128)(2,1)S(1)} %collective-permute-done.4) | copy-start | bytes 196612
  64.2 7.2 %collective-permute-start.5 = (bf16[32,1024]{1,0:T(8,128)(2,1)S(1)}, bf16[32,1024]{1,0:T(8,128)(2,1)}, u32[]{:S(2)}, u32[]{:S(2)}) collective-permute-start(bf16[32,1024]{1,0:T(8,128)(2,1)S(1)} %collective-permute-done.4), channel_id=1, source_target_pairs={{0,1},{1,2},{2,3},{3,4},{4,5},{5,6},{6,7},{7,8},{8,9},{9,10},{10,1... | collective-permute-start | bytes 196616 | tf_op jit(solution)/shard_map/ppermute | solution.py:22
  66.4 6.5 %copy-start.33 = (bf16[32,1024]{1,0:T(8,128)(2,1)}, bf16[32,1024]{1,0:T(8,128)(2,1)S(1)}, u32[]{:S(2)}) copy-start(bf16[32,1024]{1,0:T(8,128)(2,1)S(1)} %collective-permute-done.22) | copy-start | bytes 196612
  66.4 6.5 %collective-permute-start.23 = (bf16[32,1024]{1,0:T(8,128)(2,1)S(1)}, bf16[32,1024]{1,0:T(8,128)(2,1)}, u32[]{:S(2)}, u32[]{:S(2)}) collective-permute-start(bf16[32,1024]{1,0:T(8,128)(2,1)S(1)} %collective-permute-done.22), channel_id=1, source_target_pairs={{0,1},{1,2},{2,3},{3,4},{4,5},{5,6},{6,7},{7,8},{8,9},{9,10},{10,1... | collective-permute-start | bytes 196616 | tf_op jit(solution)/shard_map/ppermute | solution.py:22
  66.5 143.3 %reduce-scatter.11.cloned.1.call-start = ((), (), s32[]{:S(2)}) async-start(), calls=%async_computation.9 | async-start | bytes 2228224 | tf_op jit(solution)/shard_map/reduce_scatter | solution.py:92
  66.5 19.0 %copy-start.23 = (bf16[32,1024]{1,0:T(8,128)(2,1)S(1)}, bf16[32,1024]{1,0:T(8,128)(2,1)}, u32[]{:S(2)}) copy-start(bf16[32,1024]{1,0:T(8,128)(2,1)} %param.11) | copy-start | bytes 196612
  66.5 25.5 %copy-start.24 = (bf16[32,1024]{1,0:T(8,128)(2,1)S(1)}, bf16[32,1024]{1,0:T(8,128)(2,1)}, u32[]{:S(2)}) copy-start(bf16[32,1024]{1,0:T(8,128)(2,1)} %param.13) | copy-start | bytes 196612
  66.6 7.8 %collective-permute-start.30 = (bf16[32,1024]{1,0:T(8,128)(2,1)}, bf16[32,1024]{1,0:T(8,128)(2,1)S(1)}, u32[]{:S(2)}, u32[]{:S(2)}) collective-permute-start(bf16[32,1024]{1,0:T(8,128)(2,1)} %collective-permute-done.29), channel_id=1, source_target_pairs={{0,15},{1,0},{2,1},{3,2},{4,3},{5,4},{6,5},{7,6},{8,7},{9,8},{10,9... | collective-permute-start | bytes 196616 | tf_op jit(solution)/shard_map/ppermute | solution.py:24
  71.1 7.7 %collective-permute-start.13 = (bf16[32,1024]{1,0:T(8,128)(2,1)}, bf16[32,1024]{1,0:T(8,128)(2,1)}, u32[]{:S(2)}, u32[]{:S(2)}) collective-permute-start(bf16[32,1024]{1,0:T(8,128)(2,1)} %collective-permute-done.12), channel_id=1, source_target_pairs={{0,15},{1,0},{2,1},{3,2},{4,3},{5,4},{6,5},{7,6},{8,7},{9,8},{10,9... | collective-permute-start | bytes 196616 | tf_op jit(solution)/shard_map/ppermute | solution.py:24
  71.5 7.4 %collective-permute-start.6 = (bf16[32,1024]{1,0:T(8,128)(2,1)}, bf16[32,1024]{1,0:T(8,128)(2,1)S(1)}, u32[]{:S(2)}, u32[]{:S(2)}) collective-permute-start(bf16[32,1024]{1,0:T(8,128)(2,1)} %collective-permute-done.5), channel_id=1, source_target_pairs={{0,1},{1,2},{2,3},{3,4},{4,5},{5,6},{6,7},{7,8},{8,9},{9,10},{10,1... | collective-permute-start | bytes 196616 | tf_op jit(solution)/shard_map/ppermute | solution.py:22
  72.9 6.7 %collective-permute-start.24 = (bf16[32,1024]{1,0:T(8,128)(2,1)}, bf16[32,1024]{1,0:T(8,128)(2,1)S(1)}, u32[]{:S(2)}, u32[]{:S(2)}) collective-permute-start(bf16[32,1024]{1,0:T(8,128)(2,1)} %collective-permute-done.23), channel_id=1, source_target_pairs={{0,1},{1,2},{2,3},{3,4},{4,5},{5,6},{6,7},{7,8},{8,9},{9,10},{10,1... | collective-permute-start | bytes 196616 | tf_op jit(solution)/shard_map/ppermute | solution.py:22
  73.0 8.8 %copy-start.34 = (bf16[32,1024]{1,0:T(8,128)(2,1)S(1)}, bf16[32,1024]{1,0:T(8,128)(2,1)}, u32[]{:S(2)}) copy-start(bf16[32,1024]{1,0:T(8,128)(2,1)} %copy-done.33) | copy-start | bytes 196612
  73.0 9.4 %copy-start.32 = (bf16[32,1024]{1,0:T(8,128)(2,1)S(1)}, bf16[32,1024]{1,0:T(8,128)(2,1)}, u32[]{:S(2)}) copy-start(bf16[32,1024]{1,0:T(8,128)(2,1)} %copy-done.31) | copy-start | bytes 196612
  73.0 10.0 %copy-start.28 = (bf16[32,1024]{1,0:T(8,128)(2,1)S(1)}, bf16[32,1024]{1,0:T(8,128)(2,1)}, u32[]{:S(2)}) copy-start(bf16[32,1024]{1,0:T(8,128)(2,1)} %copy-done.27) | copy-start | bytes 196612
  73.0 15.9 %copy-start.30 = (bf16[32,1024]{1,0:T(8,128)(2,1)S(1)}, bf16[32,1024]{1,0:T(8,128)(2,1)}, u32[]{:S(2)}) copy-start(bf16[32,1024]{1,0:T(8,128)(2,1)} %copy-done.29) | copy-start | bytes 196612
  73.0 16.5 %copy-start.26 = (bf16[32,1024]{1,0:T(8,128)(2,1)S(1)}, bf16[32,1024]{1,0:T(8,128)(2,1)}, u32[]{:S(2)}) copy-start(bf16[32,1024]{1,0:T(8,128)(2,1)} %copy-done.25) | copy-start | bytes 196612
  74.3 29.7 %copy-start.9 = (bf16[2,256,1024]{2,1,0:T(8,128)(2,1)}, bf16[2,256,1024]{2,1,0:T(8,128)(2,1)S(1)}, u32[]{:S(2)}) copy-start(bf16[2,256,1024]{2,1,0:T(8,128)(2,1)S(1)} %get-tuple-element.13) | copy-start | bytes 3145732
  74.3 26.9 %collective-permute-start.31 = (bf16[32,1024]{1,0:T(8,128)(2,1)S(1)}, bf16[32,1024]{1,0:T(8,128)(2,1)S(1)}, u32[]{:S(2)}, u32[]{:S(2)}) collective-permute-start(bf16[32,1024]{1,0:T(8,128)(2,1)S(1)} %collective-permute-done.30), channel_id=1, source_target_pairs={{0,15},{1,0},{2,1},{3,2},{4,3},{5,4},{6,5},{7,6},{8,7},{9,8},{10,9... | collective-permute-start | bytes 196616 | tf_op jit(solution)/shard_map/ppermute | solution.py:24
  78.8 40.0 %collective-permute-start.14 = (bf16[32,1024]{1,0:T(8,128)(2,1)}, bf16[32,1024]{1,0:T(8,128)(2,1)}, u32[]{:S(2)}, u32[]{:S(2)}) collective-permute-start(bf16[32,1024]{1,0:T(8,128)(2,1)} %collective-permute-done.13), channel_id=1, source_target_pairs={{0,15},{1,0},{2,1},{3,2},{4,3},{5,4},{6,5},{7,6},{8,7},{9,8},{10,9... | collective-permute-start | bytes 196616 | tf_op jit(solution)/shard_map/ppermute | solution.py:24
  78.8 7.4 %collective-permute-start.7 = (bf16[32,1024]{1,0:T(8,128)(2,1)S(1)}, bf16[32,1024]{1,0:T(8,128)(2,1)S(1)}, u32[]{:S(2)}, u32[]{:S(2)}) collective-permute-start(bf16[32,1024]{1,0:T(8,128)(2,1)S(1)} %collective-permute-done.6), channel_id=1, source_target_pairs={{0,1},{1,2},{2,3},{3,4},{4,5},{5,6},{6,7},{7,8},{8,9},{9,10},{10,1... | collective-permute-start | bytes 196616 | tf_op jit(solution)/shard_map/ppermute | solution.py:22
  109.4 10.8 %copy-start.20 = (bf16[512,1024]{1,0:T(8,128)(2,1)}, bf16[512,1024]{1,0:T(8,128)(2,1)S(1)}, u32[]{:S(2)}) copy-start(bf16[512,1024]{1,0:T(8,128)(2,1)S(1)} %get-tuple-element.27) | copy-start | bytes 3145732
  113.8 24.0 %collective-permute-start.32 = (bf16[2,128,1024]{2,1,0:T(8,128)(2,1)}, bf16[2,128,1024]{2,1,0:T(8,128)(2,1)}, u32[]{:S(2)}, u32[]{:S(2)}) collective-permute-start(bf16[2,128,1024]{2,1,0:T(8,128)(2,1)} %get-tuple-element.10), channel_id=1, source_target_pairs={{0,2},{2,4},{4,6},{6,8},{8,10},{10,12},{12,14},{1,3},{3,5},{5,7},{... | collective-permute-start | bytes 1572872 | tf_op jit(solution)/shard_map/ppermute | solution.py:37
  115.8 22.0 %collective-permute-start.33 = (bf16[2,128,1024]{2,1,0:T(8,128)(2,1)}, bf16[2,128,1024]{2,1,0:T(8,128)(2,1)}, u32[]{:S(2)}, u32[]{:S(2)}) collective-permute-start(bf16[2,128,1024]{2,1,0:T(8,128)(2,1)} %get-tuple-element.11), channel_id=1, source_target_pairs={{2,0},{4,2},{6,4},{8,6},{10,8},{12,10},{14,12},{3,1},{5,3},{7,5},{... | collective-permute-start | bytes 1572872 | tf_op jit(solution)/shard_map/ppermute | solution.py:40
  120.2 17.6 %copy-start.6 = (bf16[2,256,1024]{2,1,0:T(8,128)(2,1)S(1)}, bf16[2,256,1024]{2,1,0:T(8,128)(2,1)}, u32[]{:S(2)}) copy-start(bf16[2,256,1024]{2,1,0:T(8,128)(2,1)} %copy-done.5) | copy-start | bytes 3145732
  122.6 16.6 %copy-start.14 = (bf16[1024,3,512]{2,0,1:T(8,128)(2,1)S(1)}, bf16[1024,3,512]{2,0,1:T(8,128)(2,1)}, u32[]{:S(2)}) copy-start(bf16[1024,3,512]{2,0,1:T(8,128)(2,1)} %all-gather.5.cloned.1.call-done) | copy-start | bytes 9437188
  144.0 127.8 %reduce-scatter.7.cloned.1.call-start = ((), (), s32[]{:S(2)}) async-start(), calls=%async_computation.7 | async-start | bytes 2228224 | tf_op jit(solution)/shard_map/reduce_scatter | solution.py:92
  144.0 9.2 %copy-start.15 = (bf16[1024,3,512]{2,0,1:T(8,128)(2,1)S(1)}, bf16[1024,3,512]{2,0,1:T(8,128)(2,1)}, u32[]{:S(2)}) copy-start(bf16[1024,3,512]{2,0,1:T(8,128)(2,1)} %all-gather.5.cloned.1.call-done) | copy-start | bytes 9437188
  147.5 14.7 %collective-permute-start.35 = (bf16[2,128,512]{2,1,0:T(8,128)(2,1)S(1)}, bf16[2,128,512]{2,1,0:T(8,128)(2,1)S(1)}, u32[]{:S(2)}, u32[]{:S(2)}) collective-permute-start(bf16[2,128,512]{2,1,0:T(8,128)(2,1)S(1)} %get-tuple-element.22), channel_id=1, source_target_pairs={{0,2},{2,4},{4,6},{6,8},{8,10},{10,12},{12,14},{1,3},{3,5},{5,7},{... | collective-permute-start | bytes 786440 | tf_op jit(solution)/shard_map/ppermute | solution.py:37
  151.9 10.3 %collective-permute-start.34 = (bf16[2,128,512]{2,1,0:T(8,128)(2,1)S(1)}, bf16[2,128,512]{2,1,0:T(8,128)(2,1)S(1)}, u32[]{:S(2)}, u32[]{:S(2)}) collective-permute-start(bf16[2,128,512]{2,1,0:T(8,128)(2,1)S(1)} %get-tuple-element.23), channel_id=1, source_target_pairs={{2,0},{4,2},{6,4},{8,6},{10,8},{12,10},{14,12},{3,1},{5,3},{7,5},{... | collective-permute-start | bytes 786440 | tf_op jit(solution)/shard_map/ppermute | solution.py:40
  166.9 4.8 %copy-start.17 = (f32[512,512]{1,0:T(8,128)S(1)}, f32[512,512]{1,0:T(8,128)}, u32[]{:S(2)}) copy-start(f32[512,512]{1,0:T(8,128)} %copy-done.16) | copy-start | bytes 3145732
  173.9 186.5 %reduce-scatter.9.cloned.1.call-start = ((), (), s32[]{:S(2)}) async-start(), calls=%async_computation.8 | async-start | bytes 6684672 | tf_op jit(solution)/shard_map/reduce_scatter | solution.py:102
  181.8 267.9 %reduce-scatter.5.cloned.1.call-start = ((), (), s32[]{:S(2)}) async-start(), calls=%async_computation.6 | async-start | bytes 6684672 | tf_op jit(solution)/shard_map/reduce_scatter | solution.py:102
  182.1 3.4 copy-start.10
  191.7 7.9 %collective-permute-start.37 = (bf16[2,64,512]{2,1,0:T(8,128)(2,1)S(1)}, bf16[2,64,512]{2,1,0:T(8,128)(2,1)S(1)}, u32[]{:S(2)}, u32[]{:S(2)}) collective-permute-start(bf16[2,64,512]{2,1,0:T(8,128)(2,1)S(1)} %get-tuple-element.18), channel_id=1, source_target_pairs={{0,2},{2,4},{4,6},{6,8},{8,10},{10,12},{12,14},{1,3},{3,5},{5,7},{... | collective-permute-start | bytes 393224 | tf_op jit(solution)/shard_map/ppermute | solution.py:37
  196.1 7.2 %copy-start.8 = (bf16[1024,3,512]{2,0,1:T(8,128)(2,1)S(1)}, bf16[1024,3,512]{2,0,1:T(8,128)(2,1)}, u32[]{:S(2)}) copy-start(bf16[1024,3,512]{2,0,1:T(8,128)(2,1)} %all-gather.3.cloned.1.call-done) | copy-start | bytes 9437188
  196.1 7.1 %collective-permute-start.36 = (bf16[2,64,512]{2,1,0:T(8,128)(2,1)S(1)}, bf16[2,64,512]{2,1,0:T(8,128)(2,1)S(1)}, u32[]{:S(2)}, u32[]{:S(2)}) collective-permute-start(bf16[2,64,512]{2,1,0:T(8,128)(2,1)S(1)} %get-tuple-element.19), channel_id=1, source_target_pairs={{2,0},{4,2},{6,4},{8,6},{10,8},{12,10},{14,12},{3,1},{5,3},{7,5},{... | collective-permute-start | bytes 393224 | tf_op jit(solution)/shard_map/ppermute | solution.py:40
  (15 other events, 23.1 us)
Sparse Core Ops, SparseCore 0:
  10.2 58.8 all-gather.2
  71.3 44.7 all-gather.4
  144.1 62.0 reduce-scatter.10
  210.8 60.8 reduce-scatter.6
  276.1 84.2 reduce-scatter.8
  365.3 84.3 reduce-scatter.4
